TPU v7x, 128 devices: a whole 4x4x4 slice. The times are simulated.
128 devices in a mesh: seq: 32 (over y, z, core), head: 4 (over x).
Axes of the slice: x: 4, y: 4, z: 4, core: 2. Of those that a mesh axis runs over, the one named last changes fastest.
Arguments:
- queries: bfloat16 [131072, 2048], P('seq', 'head'), may hold values from -6 to 6
- keys: bfloat16 [131072, 2048], P('seq', 'head'), may hold values from -0.59765625 to 0.59765625
- values: bfloat16 [131072, 2048], P('seq', 'head'), may hold values from -6 to 6
- norm_gain: float32 [2048], replicated, may hold values from 0.1 to 1.9
Outputs:
- normed: bfloat16 [131072, 2048], P(('seq', 'head'))
All inputs are finite; a program needn't handle non-finite values.
Results may differ from a plain program's by a relative error of at most 0.0058.
Values may be sent and summed in bfloat16 or wider, within the bound.
A program may use at most 128 MiB of HBM per device.

v0:
```python
import jax
import jax.numpy as jnp
from jax import lax
from jax.sharding import PartitionSpec as P

DH = 128
BLK = 512


def add_lower(piece, mine):
    ranks = jnp.arange(piece.shape[0], dtype=jnp.int32)
    keep = (ranks < mine).astype(jnp.float32)[:, None, None, None]
    return jnp.sum(piece * keep, axis=0)


def shards(queries, keys, values, norm_gain):
    rows, width = queries.shape
    heads = width // DH
    blocks = rows // BLK
    query_rows = queries.reshape(blocks, BLK, heads, DH)
    key_rows = keys.reshape(blocks, BLK, heads, DH)
    value_rows = values.reshape(blocks, BLK, heads, DH)
    block_state = jnp.einsum(
        "nbhd,nbhe->nhde", key_rows, value_rows, preferred_element_type=jnp.float32
    )
    total = jnp.sum(block_state, axis=0)
    mine = lax.axis_index("seq")
    before = add_lower(lax.all_gather(total[None], "seq", axis=0, tiled=True), mine)
    running = jnp.cumsum(block_state, axis=0)
    within = jnp.concatenate([jnp.zeros_like(block_state[:1]), running[:-1]], axis=0)
    prefix_low = (before[None] + within).astype(jnp.bfloat16)
    inter = jnp.einsum(
        "nbhd,nhde->nbhe", query_rows, prefix_low, preferred_element_type=jnp.float32
    )
    scores = jnp.einsum("nbhd,nchd->nhbc", query_rows, key_rows, preferred_element_type=jnp.float32)
    causal = jnp.arange(BLK)[:, None] >= jnp.arange(BLK)[None, :]
    scores = jnp.where(causal[None, None], scores, jnp.zeros_like(scores)).astype(jnp.bfloat16)
    intra = jnp.einsum("nhbc,nche->nbhe", scores, value_rows, preferred_element_type=jnp.float32)
    attention = (inter + intra).astype(jnp.bfloat16).reshape(rows, width)
    regrouped = lax.all_to_all(attention, "head", split_axis=0, concat_axis=1, tiled=True)
    widened = regrouped.astype(jnp.float32)
    meansq = jnp.mean(widened * widened, axis=-1, keepdims=True)
    return (widened * lax.rsqrt(meansq + 1e-06) * norm_gain[None, :]).astype(jnp.bfloat16)


def solution(mesh):
    return jax.shard_map(
        shards,
        mesh=mesh,
        in_specs=(P("seq", "head"), P("seq", "head"), P("seq", "head"), P()),
        out_specs=P(("seq", "head"), None),
        check_vma=False,
    )
```

profile of v0, /device:TPU:1, one launch (start us, length us, event | category | flops | bytes accessed | tf_op | source)
XLA Modules:
  0.0 208.3 jit_solution(7834512053648835471)
XLA Ops:
  6.5 0.0 all-gather.3.cloned.1.call-start
  6.5 6.9 %reshape.43 = bf16[8,512,4,128]{3,2,1,0:T(4,128)(2,1)} reshape(bf16[4096,512]{1,0:T(8,128)(2,1)} %param.5) | data formatting | bytes 8388608 | tf_op jit(solution)/shard_map/reshape | solution.py:21
  13.4 6.9 %reshape.44 = bf16[8,512,4,128]{3,2,1,0:T(4,128)(2,1)} reshape(bf16[4096,512]{1,0:T(8,128)(2,1)} %param.6) | data formatting | bytes 8388608 | tf_op jit(solution)/shard_map/reshape | solution.py:22
  20.4 5.9 %fusion.28 = (f32[4,128,128]{2,1,0:T(8,128)}, f32[8,4,128,128]{3,2,1,0:T(8,128)S(1)}) fusion(bf16[8,512,4,128]{3,2,1,0:T(4,128)(2,1)} %reshape.44, bf16[8,512,4,128]{3,2,1,0:T(4,128)(2,1)} %reshape.43), kind=kOutput, calls=%fused_computation.29 | convolution fusion | flops 537329664 | bytes 10747904 | tf_op jit(solution)/shard_map/nbhd,nbhe->nhde/dot_general | solution.py:23
  26.3 0.0 all-gather.3.cloned.1.call-update
  26.3 6.9 %reshape.45 = bf16[8,512,4,128]{3,2,1,0:T(4,128)(2,1)} reshape(bf16[4096,512]{1,0:T(8,128)(2,1)} %param.4) | data formatting | bytes 8388608 | tf_op jit(solution)/shard_map/reshape | solution.py:20
  33.2 1.9 fusion.29
  35.1 0.2 slice.4
  35.3 0.1 iota_compare_fusion
  35.4 47.7 %all-gather.3.cloned.1.call-done = f32[128,128,128]{2,1,0:T(8,128)} async-done(((f32[4,128,128]{2,1,0:T(8,128)}), f32[128,128,128]{2,1,0:T(8,128)}) %all-gather.3.cloned.1.call-update) | async-done | bytes 8388624 | tf_op jit(solution)/shard_map/all_gather | solution.py:28
  83.1 0.0 copy-start
  83.1 4.7 %multiply_reduce_fusion = f32[4,128,128]{2,1,0:T(8,128)S(1)} fusion(f32[32,4,128,128]{3,2,1,0:T(8,128)} %bitcast.16, f32[32]{0:T(128)S(1)} %compare_convert_fusion), kind=kLoop, calls=%fused_computation.13 | loop fusion | flops 4128768 | bytes 8650880 | tf_op jit(solution)/shard_map/reduce_sum | solution.py:13
  87.8 0.0 copy-done
  87.8 4.6 %fusion.15 = f32[8,4,128,512]{3,2,1,0:T(8,128)} fusion(bf16[8,512,4,128]{3,2,1,0:T(4,128)(2,1)S(1)} %copy-done, f32[7,4,128,128]{3,2,1,0:T(8,128)S(1)} %slice.4, f32[4,128,128]{2,1,0:T(8,128)S(1)} %multiply_reduce_fusion), kind=kOutput, calls=%fused_computation.18 | convolution fusion | flops 537919488 | bytes 14680064 | tf_op jit(solution)/shard_map/nbhd,nhde->nbhe/dot_general | solution.py:32
  92.4 16.4 %fusion.8 = bf16[8,512,4,128]{1,3,2,0:T(8,128)(2,1)} fusion(f32[8,4,128,512]{3,2,1,0:T(8,128)} %fusion.15, bf16[8,512,4,128]{3,2,1,0:T(4,128)(2,1)} %reshape.44, pred[512,512]{1,0:T(8,128)(4,1)S(1)} %iota_compare_fusion, bf16[8,512,4,128]{3,2,1,0:T(4,128)(2,1)} %reshape.43, bf16[8,512,4,128]{3,2,1,0:T(4,128)(2,1)} %reshape.45), kind=kOutput, calls=%fused_computation.12 | convolution fusion | flops 4315938816 | bytes 25427968 | tf_op jit(solution)/shard_map/nhbc,nche->nbhe/dot_general | solution.py:38
  108.9 7.4 %copy.37 = bf16[8,512,4,128]{3,2,1,0:T(4,128)(2,1)} copy(bf16[8,512,4,128]{1,3,2,0:T(8,128)(2,1)} %fusion.8) | data formatting | bytes 8388608 | tf_op jit(solution)/shard_map/convert_element_type | solution.py:39
  116.3 7.2 %all_to_all.10 = bf16[4,1024,512]{2,1,0:T(8,128)(2,1)} reshape(bf16[8,512,4,128]{3,2,1,0:T(4,128)(2,1)} %copy.37) | data formatting | bytes 8388608 | tf_op jit(solution)/shard_map/all_to_all | solution.py:40
  123.5 52.3 %all_to_all.13 = bf16[4,1024,512]{2,1,0:T(8,128)(2,1)S(1)} all-to-all(bf16[4,1024,512]{2,1,0:T(8,128)(2,1)} %all_to_all.10), channel_id=1, replica_groups=mesh['seq'=32,'head'=4] {'head'}, dimensions={0} | all-to-all | bytes 8388608 | tf_op jit(solution)/shard_map/all_to_all | solution.py:40
  175.8 0.9 fusion.5
  176.7 4.4 %convert_bitcast_fusion = f32[1024,4,512]{2,0,1:T(8,128)} fusion(bf16[4,1024,512]{2,1,0:T(8,128)(2,1)S(1)} %all_to_all.13), kind=kLoop, calls=%fused_computation.6 | loop fusion | flops 2097152 | bytes 12582912 | tf_op jit(solution)/shard_map/convert_element_type | solution.py:41
  181.1 0.0 copy-start.1
  181.1 8.7 %copy.38 = f32[1024,4,512]{0,2,1:T(8,128)} copy(f32[1024,4,512]{2,0,1:T(8,128)} %convert_bitcast_fusion) | data formatting | bytes 16777216 | tf_op jit(solution)/shard_map/convert_element_type | solution.py:41
  189.9 0.0 copy-done.1
  189.9 5.2 %fusion.7 = bf16[1024,2048]{0,1:T(8,128)(2,1)} fusion(f32[1024,4,512]{0,2,1:T(8,128)} %copy.38, f32[2048]{0:T(1024)S(1)} %copy-done.1, f32[1024]{0:T(1024)S(1)} %add_rsqrt_fusion), kind=kLoop, calls=%fused_computation.10 | loop fusion | flops 6291456 | bytes 12595200 | tf_op jit(solution)/shard_map/convert_element_type | solution.py:43
  195.1 6.4 %copy.39 = bf16[1024,2048]{1,0:T(8,128)(2,1)} copy(bf16[1024,2048]{0,1:T(8,128)(2,1)} %fusion.7) | data formatting | bytes 8388608 | tf_op jit(solution)/shard_map/convert_element_type | solution.py:43
  (2 shorter events, 0.0 us)
Async XLA Ops:
  6.5 76.6 %all-gather.3.cloned.1.call-start = ((), (), s32[]{:S(2)}) async-start(), calls=%async_computation.1 | async-start | bytes 8650752 | tf_op jit(solution)/shard_map/all_gather | solution.py:28
  83.1 4.7 %copy-start = (bf16[8,512,4,128]{3,2,1,0:T(4,128)(2,1)S(1)}, bf16[8,512,4,128]{3,2,1,0:T(4,128)(2,1)}, u32[]{:S(2)}) copy-start(bf16[8,512,4,128]{3,2,1,0:T(4,128)(2,1)} %reshape.45) | copy-start | bytes 12582916
  181.1 8.8 %copy-start.1 = (f32[2048]{0:T(1024)S(1)}, f32[2048]{0:T(1024)}, u32[]{:S(2)}) copy-start(f32[2048]{0:T(1024)} %param.7) | copy-start | bytes 24580
Sparse Core Ops, SparseCore 0:
  26.4 56.6 all-gather.2
where the time goes:
time: 210 us; the launch traced here: 208 us
  blocking collectives  52.3 us (25%)
  local copies, waits for them, and re-layouts  50.7 us (24%)
  waiting for transfers between devices  47.7 us (23%)
  matrix products  27 us (13%)
  other arithmetic  17.1 us (8%)
  between operations  13.5 us (6%)
    all_to_all x1, blocking collectives, shards(): lax.all_to_all(attention, 'head', split_axis=0, concat_axis=1, tiled=True)  52.3 us
    all_gather x1, waiting for transfers between devices, shards(): lax.all_gather(total[None], 'seq', axis=0, tiled=True)  47.7 us
    dot_general x1, matrix products, shards(): jnp.einsum('nhbc,nche->nbhe', scores, value_rows, preferred_element_type=...  16.4 us
    convert_element_type x1, local copies, waits for them, and re-layouts, shards(): widened = regrouped.astype(jnp.float32)  8.75 us
    convert_element_type x1, local copies, waits for them, and re-layouts, shards(): attention = (inter + intra).astype(jnp.bfloat16).reshape(rows, width)  7.44 us
    all_to_all x1, local copies, waits for them, and re-layouts, shards(): lax.all_to_all(attention, 'head', split_axis=0, concat_axis=1, tiled=True)  7.21 us
    reshape x1, local copies, waits for them, and re-layouts, shards(): value_rows = values.reshape(blocks, BLK, heads, DH)  6.93 us
    reshape x1, local copies, waits for them, and re-layouts, shards(): key_rows = keys.reshape(blocks, BLK, heads, DH)  6.91 us
  transfers between devices with their start and end apart: 1, of which 1 were waited for; matrix products, arithmetic and copies ran while one was open for 4% of the time, Pallas kernels for 0%

commit v1 on v0

v1 whole, which is shorter than its diff:
```python
import jax
import jax.numpy as jnp
from jax import lax
from jax.experimental import pallas as pl
from jax.experimental.pallas import tpu as pltpu
from jax.sharding import PartitionSpec as P

DH = 128
BLK = 512
HALF = BLK // 2
MESH = pl.DeviceIdType.MESH
F32 = jnp.float32
BF16 = jnp.bfloat16


def dot(a, b, dims):
    return lax.dot_general(a, b, (dims, ((), ())), preferred_element_type=F32)


def make_kernel(seqs, groups, rows, width):
    heads = width // DH
    blocks = rows // BLK
    own = rows // groups
    part = (heads * DH) // seqs
    per = own // BLK
    pieces = own // HALF
    sending = (groups - 1) * per

    def kernel(q_hbm, k_hbm, v_hbm, g_ref, o_hbm, q, k, v, st, tot, got, pre, before, acc, att, rcv,
               in_sem, out_sem, scan_send, scan_recv, send_sem, recv_sem):
        me = lax.axis_index("head")
        my = lax.axis_index("seq")

        def load(i, n):
            hbm, ref = ((k_hbm, k), (v_hbm, v), (q_hbm, q))[i]
            sl = pl.ds(pl.multiple_of(n * BLK, BLK), BLK)
            return pltpu.make_async_copy(hbm.at[sl], ref.at[sl], in_sem.at[i, n])

        for n in range(blocks):
            load(0, n).start()
            load(1, n).start()
        for n in range(blocks):
            load(2, n).start()

        barrier = pltpu.get_barrier_semaphore()

        @pl.loop(1, seqs)
        def _(i):
            pl.semaphore_signal(barrier, inc=1, device_id={"seq": lax.rem(my + i, seqs)}, device_id_type=MESH)

        for d in range(1, groups):
            pl.semaphore_signal(barrier, inc=1, device_id={"head": lax.rem(me + d, groups)}, device_id_type=MESH)

        tot[...] = jnp.zeros_like(tot)

        @pl.loop(0, blocks)
        def _(n):
            load(0, n).wait()
            load(1, n).wait()
            sl = pl.ds(pl.multiple_of(n * BLK, BLK), BLK)
            for h in range(heads):
                hs = slice(h * DH, (h + 1) * DH)
                state = dot(k[sl, hs], v[sl, hs], ((0,), (0,)))
                run = tot[hs, :]
                st[n, hs, :] = run
                tot[hs, :] = run + state

        pl.semaphore_wait(barrier, seqs - 1 + groups - 1)

        def mine(i):
            return pl.ds(pl.multiple_of(i * part, part), part)

        def first(i):
            return pltpu.make_async_remote_copy(
                src_ref=tot.at[mine(i)], dst_ref=got.at[my], send_sem=scan_send.at[0], recv_sem=scan_recv.at[0],
                device_id={"seq": i}, device_id_type=MESH)

        def second(i):
            return pltpu.make_async_remote_copy(
                src_ref=pre.at[i], dst_ref=before.at[mine(my)], send_sem=scan_send.at[1], recv_sem=scan_recv.at[1],
                device_id={"seq": i}, device_id_type=MESH)

        def all_of(stage):
            ref = got.at[pl.ds(0, seqs - 1)]
            return pltpu.make_async_remote_copy(
                src_ref=ref, dst_ref=ref, send_sem=scan_send.at[stage], recv_sem=scan_recv.at[stage],
                device_id={"seq": lax.rem(my + 1, seqs)}, device_id_type=MESH)

        @pl.loop(1, seqs)
        def _(i):
            first(lax.rem(my + i, seqs)).start()

        got[my] = tot[mine(my), :]

        row = lax.broadcasted_iota(jnp.int32, (HALF, HALF), 0)
        col = lax.broadcasted_iota(jnp.int32, (HALF, HALF), 1)
        causal = row >= col

        def step_of(j):
            i = lax.rem(j, groups - 1)
            d = jnp.where(j < sending, 1 + lax.rem(2 * i, groups - 1), 0)
            piece = jnp.where(j < sending, j // (groups - 1), j - sending)
            dest = lax.rem(me + d, groups)
            return d, piece, dest, dest * per + piece

        def local(j):
            _, _, _, n = step_of(j)
            lo = pl.ds(pl.multiple_of(n * BLK, BLK), HALF)
            hi = pl.ds(pl.multiple_of(n * BLK + HALF, HALF), HALF)
            for h in range(heads):
                hs = slice(h * DH, (h + 1) * DH)
                k_lo, k_hi, v_lo, v_hi = k[lo, hs], k[hi, hs], v[lo, hs], v[hi, hs]
                q_lo, q_hi = q[lo, hs], q[hi, hs]
                s = jnp.where(causal, dot(q_lo, k_lo, ((1,), (1,))), 0.0).astype(BF16)
                acc[lo, hs] = dot(s, v_lo, ((1,), (0,)))
                s_l = dot(q_hi, k_lo, ((1,), (1,))).astype(BF16)
                s_h = jnp.where(causal, dot(q_hi, k_hi, ((1,), (1,))), 0.0).astype(BF16)
                acc[hi, hs] = dot(s_l, v_lo, ((1,), (0,))) + dot(s_h, v_hi, ((1,), (0,)))

        for n in range(blocks):
            load(2, n).wait()

        @pl.loop(0, sending // 2)
        def _(j):
            local(j)

        all_of(0).wait_recv()
        run = jnp.zeros((part, DH), F32)
        for i in range(seqs):
            pre[i] = run
            run = run + got[i]

        @pl.loop(1, seqs)
        def _(i):
            second(lax.rem(my + i, seqs)).start()

        before[mine(my), :] = pre[my]

        @pl.loop(sending // 2, sending)
        def _(j):
            local(j)

        all_of(1).wait_recv()

        def exchange(d, n, half):
            dest = lax.rem(me + d, groups)
            to = pl.ds(pl.multiple_of((n - dest * per) * BLK + half * HALF, HALF), HALF)
            at = pl.ds(pl.multiple_of(n * BLK + half * HALF, HALF), HALF)
            piece = (n - dest * per) * 2 + half
            return pltpu.make_async_remote_copy(
                src_ref=att.at[at], dst_ref=rcv.at[to, pl.ds(pl.multiple_of(me * width, width), width)],
                send_sem=send_sem.at[d, piece], recv_sem=recv_sem.at[d, piece],
                device_id={"head": dest}, device_id_type=MESH)

        def arrival(d, piece):
            src = lax.rem(me + groups - d, groups)
            at = pl.ds(pl.multiple_of(piece * HALF, HALF), HALF)
            return pltpu.make_async_remote_copy(
                src_ref=att.at[at], dst_ref=rcv.at[at, pl.ds(pl.multiple_of(src * width, width), width)],
                send_sem=send_sem.at[d, piece], recv_sem=recv_sem.at[d, piece],
                device_id={"head": src}, device_id_type=MESH)

        def rows_of(n, half, h):
            at = pl.ds(pl.multiple_of(n * BLK + half * HALF, HALF), HALF)
            hs = slice(h * DH, (h + 1) * DH)
            low = (before[hs, :] + st[n, hs, :]).astype(BF16)
            return (acc[at, hs] + dot(q[at, hs], low, ((1,), (0,)))).astype(BF16)

        @pl.loop(0, sending)
        def _(j):
            d, _, _, n = step_of(j)
            for half in range(2):
                at = pl.ds(pl.multiple_of(n * BLK + half * HALF, HALF), HALF)
                for h in range(heads):
                    att[at, h * DH:(h + 1) * DH] = rows_of(n, half, h)
                exchange(d, n, half).start()

        @pl.loop(sending, blocks)
        def _(j):
            _, piece, _, n = step_of(j)
            local(j)
            for half in range(2):
                to = pl.ds(pl.multiple_of(piece * BLK + half * HALF, HALF), HALF)
                for h in range(heads):
                    rcv[to, pl.ds(pl.multiple_of(me * width + h * DH, DH), DH)] = rows_of(n, half, h)

        def store(piece):
            at = pl.ds(pl.multiple_of(piece * HALF, HALF), HALF)
            return pltpu.make_async_copy(rcv.at[at], o_hbm.at[at], out_sem.at[piece])

        @pl.loop(0, pieces)
        def _(piece):
            for d in range(1, groups):
                arrival(d, piece).wait_recv()

            @pl.loop(0, HALF // 32)
            def _(i):
                at = pl.ds(pl.multiple_of(piece * HALF + i * 32, 32), 32)
                wide = rcv[at, :].astype(F32)
                mean = jnp.mean(wide * wide, axis=-1, keepdims=True)
                rcv[at, :] = (wide * lax.rsqrt(mean + 1e-06) * g_ref[...]).astype(BF16)

            store(piece).start()

        @pl.loop(0, pieces)
        def _(piece):
            store(piece).wait()
            for d in range(1, groups):
                arrival(d, piece).wait_send()

        all_of(0).wait_send()
        all_of(1).wait_send()

    return kernel


def solution(mesh):
    seqs, groups = mesh.shape["seq"], mesh.shape["head"]

    def shards(queries, keys, values, norm_gain):
        rows, width = queries.shape
        heads = width // DH
        blocks = rows // BLK
        own = rows // groups
        full = width * groups
        part = width // seqs
        any_spec = pl.BlockSpec(memory_space=pl.ANY)
        return pl.pallas_call(
            make_kernel(seqs, groups, rows, width),
            out_shape=jax.ShapeDtypeStruct((own, full), BF16),
            in_specs=[any_spec] * 3 + [pl.BlockSpec(memory_space=pltpu.VMEM)],
            out_specs=any_spec,
            scratch_shapes=[
                pltpu.VMEM((rows, width), BF16),
                pltpu.VMEM((rows, width), BF16),
                pltpu.VMEM((rows, width), BF16),
                pltpu.VMEM((blocks, width, DH), F32),
                pltpu.VMEM((width, DH), F32),
                pltpu.VMEM((seqs, part, DH), F32),
                pltpu.VMEM((seqs, part, DH), F32),
                pltpu.VMEM((width, DH), F32),
                pltpu.VMEM((rows, width), F32),
                pltpu.VMEM((rows, width), BF16),
                pltpu.VMEM((own, full), BF16),
                pltpu.SemaphoreType.DMA((3, blocks)),
                pltpu.SemaphoreType.DMA((own // HALF,)),
                pltpu.SemaphoreType.DMA((2,)),
                pltpu.SemaphoreType.DMA((2,)),
                pltpu.SemaphoreType.DMA((groups, own // HALF)),
                pltpu.SemaphoreType.DMA((groups, own // HALF)),
            ],
            compiler_params=pltpu.CompilerParams(
                collective_id=0, has_side_effects=True, vmem_limit_bytes=56 << 20),
            name="attention_norm",
        )(queries, keys, values, norm_gain[None, :])

    return jax.shard_map(
        shards,
        mesh=mesh,
        in_specs=(P("seq", "head"), P("seq", "head"), P("seq", "head"), P()),
        out_specs=P(("seq", "head"), None),
        check_vma=False,
    )
```

time: 210 us -> 77.7 us (0.37)
  Pallas kernels: 0 us -> 72.7 us
  blocking collectives: 52.3 us -> 0 us
  waiting for transfers between devices: 47.7 us -> 0 us
  local copies, waits for them, and re-layouts: 50.7 us -> 4.79 us
  matrix products: 27 us -> 0 us
  other arithmetic: 17.1 us -> 0 us
  between operations: 13.5 us -> 0.01 us
    pallas_call x0 -> x1, Pallas kernels: none -> 72.7 us  [shards(): pl.pallas_call(make_kernel(seqs, groups, rows, width), out_shape=jax.Shap...]
    all_to_all x1 -> x0, blocking collectives: 52.3 us -> none  [shards(): lax.all_to_all(attention, 'head', split_axis=0, concat_axis=1, tiled=True)]
    all_gather x1 -> x0, waiting for transfers between devices: 47.7 us -> none  [shards(): lax.all_gather(total[None], 'seq', axis=0, tiled=True)]
    dot_general x3 -> x0, matrix products: 27 us -> none  [the longest x1 16.4 us: shards(): jnp.einsum('nhbc,nche->nbhe', scores, value_rows, preferred_element_type=...]
    convert_element_type x3 -> x0, local copies, waits for them, and re-layouts: 22.6 us -> none  [the longest x1 8.75 us: shards(): widened = regrouped.astype(jnp.float32)]
    reshape x3 -> x0, local copies, waits for them, and re-layouts: 20.7 us -> none  [the longest x1 6.93 us: shards(): value_rows = values.reshape(blocks, BLK, heads, DH)]
    convert_element_type x3 -> x0, other arithmetic: 9.58 us -> none  [the longest x1 5.17 us: shards(): (widened * lax.rsqrt(meansq + 1e-06) * norm_gain[None, :]).astype(jnp.bfl...]
    all_to_all x1 -> x0, local copies, waits for them, and re-layouts: 7.21 us -> none  [shards(): lax.all_to_all(attention, 'head', split_axis=0, concat_axis=1, tiled=True)]
  transfers between devices with their start and end apart: 1 -> 0, of which waited for: 1 -> 0; matrix products, arithmetic and copies ran while one was open for 4% -> 0% of each run, Pallas kernels for 0% -> 0%
where the time goes in v1:
time: 77.7 us; the launch traced here: 77.5 us
  Pallas kernels  72.7 us (94%)
  local copies, waits for them, and re-layouts  4.79 us (6%)
    pallas_call x1, Pallas kernels, shards(): pl.pallas_call(make_kernel(seqs, groups, rows, width), out_shape=jax.Shap...  72.7 us
    unnamed x1, local copies, waits for them, and re-layouts  4.79 us

profile of v1, /device:TPU:1, one launch (start us, length us, event | category | flops | bytes accessed | tf_op | source)
XLA Modules:
  0.0 77.5 jit_solution(17355788769863663943)
XLA Ops:
  0.0 72.7 %attention_norm.1 = bf16[1024,2048]{1,0:T(8,128)(2,1)} custom-call(bf16[4096,512]{1,0:T(8,128)(2,1)} %q_hbm.1, bf16[4096,512]{1,0:T(8,128)(2,1)} %k_hbm.1, bf16[4096,512]{1,0:T(8,128)(2,1)} %v_hbm.1, f32[1,2048]{1,0:T(1,128)} %bitcast.1), custom_call_target="tpu_custom_call" | custom-call | tf_op jit(solution)/shard_map/attention_norm/pallas_call | solution.py:228
  72.7 4.8 %copy.6 = bf16[1024,2048]{1,0:T(8,128)(2,1)} copy(bf16[1024,2048]{1,0:T(8,128)(2,1)} %attention_norm.1) | data formatting | bytes 8388608

commit v2 on v1

v2 whole, which is shorter than its diff:
```python
import jax
import jax.numpy as jnp
from jax import lax
from jax.experimental import pallas as pl
from jax.experimental.pallas import tpu as pltpu
from jax.sharding import PartitionSpec as P

DH = 128
BLK = 512
HALF = BLK // 2
MESH = pl.DeviceIdType.MESH
F32 = jnp.float32
BF16 = jnp.bfloat16


def dot(a, b, dims):
    return lax.dot_general(a, b, (dims, ((), ())), preferred_element_type=F32)


def offsets(seqs):
    side = 1
    while side * side * 2 < seqs:
        side += 1
    assert side * side * 2 == seqs

    def hops(step):
        return min(step, side - step)

    steps = [(y, z, c) for y in range(side) for z in range(side) for c in range(2)]
    steps.remove((0, 0, 0))
    return side, sorted(steps, key=lambda s: (-hops(s[0]) - hops(s[1]), s))


def make_kernel(seqs, groups, rows, width):
    assert groups == 4
    heads = width // DH
    blocks = rows // BLK
    own = rows // groups
    part = (heads * DH) // seqs
    per = own // BLK
    pieces = own // HALF
    side, steps = offsets(seqs)
    later = tuple(range(1, heads))
    every = tuple(range(heads))

    def kernel(q_hbm, k_hbm, v_hbm, g_hbm, out, q, k, v, gain, st, tot, got, pre, before, acc, att, rcv,
               q_out, q_in, l_out, l_in, p_out, p_in,
               in_sem, gain_sem, scan_send, scan_recv, send_sem, recv_sem, q_sems, l_sems, p_sems):
        me = lax.axis_index("head")
        my = lax.axis_index("seq")

        def block(n):
            return pl.ds(pl.multiple_of(n * BLK, BLK), BLK)

        def half_of(n, half):
            return pl.ds(pl.multiple_of(n * BLK + half * HALF, HALF), HALF)

        def load(i, n):
            hbm, ref = ((k_hbm, k), (v_hbm, v), (q_hbm, q))[i]
            return pltpu.make_async_copy(hbm.at[block(n)], ref.at[block(n)], in_sem.at[i, n])

        for n in range(blocks):
            load(0, n).start()
            load(1, n).start()
        for n in range(blocks):
            load(2, n).start()
        load_gain = pltpu.make_async_copy(g_hbm, gain, gain_sem)
        load_gain.start()

        barrier = pltpu.get_barrier_semaphore()

        @pl.loop(1, seqs)
        def _(i):
            pl.semaphore_signal(barrier, inc=1, device_id={"seq": lax.rem(my + i, seqs)}, device_id_type=MESH)

        for d in range(1, groups):
            pl.semaphore_signal(barrier, inc=1, device_id={"head": lax.rem(me + d, groups)}, device_id_type=MESH)

        tot[...] = jnp.zeros_like(tot)

        @pl.loop(0, blocks)
        def _(n):
            load(0, n).wait()
            load(1, n).wait()
            for h in range(heads):
                hs = slice(h * DH, (h + 1) * DH)
                state = dot(k[block(n), hs], v[block(n), hs], ((0,), (0,)))
                run = tot[hs, :]
                st[n, hs, :] = run
                tot[hs, :] = run + state

        for n in range(blocks):
            load(2, n).wait()

        def first_block(d):
            return lax.rem(me + d, groups) * per

        for slot in range(2):
            at = pl.ds(pl.multiple_of(first_block(1 + 2 * slot) * BLK, BLK), own)
            q_out[slot] = q[at, :DH]

        pl.semaphore_wait(barrier, seqs - 1 + groups - 1)

        def mine(i):
            return pl.ds(pl.multiple_of(i * part, part), part)

        def first(i):
            return pltpu.make_async_remote_copy(
                src_ref=tot.at[mine(i)], dst_ref=got.at[my], send_sem=scan_send.at[0], recv_sem=scan_recv.at[0],
                device_id={"seq": i}, device_id_type=MESH)

        def second(i):
            return pltpu.make_async_remote_copy(
                src_ref=pre.at[i], dst_ref=before.at[my], send_sem=scan_send.at[1], recv_sem=scan_recv.at[1],
                device_id={"seq": i}, device_id_type=MESH)

        def all_of(stage):
            ref = (got, before)[stage].at[pl.ds(0, seqs - 1)]
            return pltpu.make_async_remote_copy(
                src_ref=ref, dst_ref=ref, send_sem=scan_send.at[stage], recv_sem=scan_recv.at[stage],
                device_id={"seq": lax.rem(my + 1, seqs)}, device_id_type=MESH)

        my_y, my_z, my_c = my // (2 * side), lax.rem(my // 2, side), lax.rem(my, 2)

        def away(step):
            y = lax.rem(my_y + step[0], side)
            z = lax.rem(my_z + step[1], side)
            return (y * side + z) * 2 + lax.rem(my_c + step[2], 2)

        for step in steps:
            first(away(step)).start()

        def ahead(src, dst, sems, slot, *which):
            return pltpu.make_async_remote_copy(
                src_ref=src, dst_ref=dst, send_sem=sems.at[(0, slot) + which], recv_sem=sems.at[(1, slot) + which],
                device_id={"head": lax.rem(me + 1 + 2 * slot, groups)}, device_id_type=MESH)

        def send_q(slot):
            return ahead(q_out.at[slot], q_in.at[slot], q_sems, slot)

        def send_l(slot, piece):
            return ahead(l_out.at[slot, block(piece)], l_in.at[slot, block(piece)], l_sems, slot, piece)

        def send_p(slot):
            return ahead(p_out, p_in.at[slot], p_sems, slot)

        for slot in range(2):
            send_q(slot).start()

        got[my] = tot[mine(my), :]

        row = lax.broadcasted_iota(jnp.int32, (HALF, HALF), 0)
        col = lax.broadcasted_iota(jnp.int32, (HALF, HALF), 1)
        causal = row >= col

        def local(n, h):
            hs = slice(h * DH, (h + 1) * DH)
            lo, hi = half_of(n, 0), half_of(n, 1)
            k_lo, k_hi, v_lo, v_hi = k[lo, hs], k[hi, hs], v[lo, hs], v[hi, hs]
            q_lo, q_hi = q[lo, hs], q[hi, hs]
            s = jnp.where(causal, dot(q_lo, k_lo, ((1,), (1,))), 0.0).astype(BF16)
            s_l = dot(q_hi, k_lo, ((1,), (1,))).astype(BF16)
            s_h = jnp.where(causal, dot(q_hi, k_hi, ((1,), (1,))), 0.0).astype(BF16)
            return (dot(s, v_lo, ((1,), (0,))),
                    dot(s_l, v_lo, ((1,), (0,))) + dot(s_h, v_hi, ((1,), (0,))))

        @pl.loop(0, 2 * per)
        def _(e):
            slot, piece = lax.rem(e, 2), e // 2
            n = first_block(1 + 2 * slot) + piece
            low = st[n, :DH, :].astype(BF16)
            for half, value in enumerate(local(n, 0)):
                value = value + dot(q[half_of(n, half), :DH], low, ((1,), (0,)))
                l_out[slot, half_of(piece, half), :] = value.astype(BF16)
            send_l(slot, piece).start()

        def keep(n, which):
            for h in which:
                hs = slice(h * DH, (h + 1) * DH)
                acc[half_of(n, 0), hs], acc[half_of(n, 1), hs] = local(n, h)

        def keep_sides(piece):
            @pl.loop(0, 2)
            def _(slot):
                keep(first_block(1 + 2 * slot) + piece, later)

        keep_sides(0)

        all_of(0).wait_recv()
        run = jnp.zeros((part, DH), F32)
        for i in range(seqs):
            pre[i] = run.astype(BF16)
            run = run + got[i]

        for step in steps:
            second(away(step)).start()

        before[my] = pre[my]

        keep(first_block(2), every)

        all_of(1).wait_recv()

        def state(n, h):
            some = slice(h * DH // part, (h + 1) * DH // part)
            old = before[some].reshape(DH, DH).astype(F32)
            return old + st[n, h * DH:(h + 1) * DH, :]

        p_out[...] = before[:DH // part].reshape(DH, DH)
        for slot in range(2):
            send_p(slot).start()

        def exchange(d, piece, half, skip, source):
            partner = lax.rem(me + (groups - d if source else d), groups)
            owner = partner if source else me
            to = half_of(piece, half)
            at = to if source else half_of(partner * per + piece, half)
            cols = pl.ds(pl.multiple_of(owner * width + skip * DH, DH), width - skip * DH)
            which = (d, piece * 2 + half)
            return pltpu.make_async_remote_copy(
                src_ref=att.at[at, pl.ds(skip * DH, width - skip * DH)], dst_ref=rcv.at[to, cols],
                send_sem=send_sem.at[which], recv_sem=recv_sem.at[which],
                device_id={"head": partner}, device_id_type=MESH)

        def rows_of(n, half, h):
            hs = slice(h * DH, (h + 1) * DH)
            at = half_of(n, half)
            low = state(n, h).astype(BF16)
            return (acc[at, hs] + dot(q[at, hs], low, ((1,), (0,)))).astype(BF16)

        def finish(d, piece, which):
            n = first_block(d) + piece
            for half in range(2):
                for h in which:
                    att[half_of(n, half), h * DH:(h + 1) * DH] = rows_of(n, half, h)
                exchange(d, piece, half, which[0], False).start()

        def finish_sides(piece):
            @pl.loop(0, 2)
            def _(slot):
                finish(1 + 2 * slot, piece, later)

        finish_sides(0)
        finish(2, 0, every)

        @pl.loop(1, per)
        def _(piece):
            keep_sides(piece)
            finish_sides(piece)
            keep(first_block(2) + piece, every)
            finish(2, piece, every)

        @pl.loop(0, per)
        def _(piece):
            n = me * per + piece
            keep(n, every)
            for half in range(2):
                for h in every:
                    cols = pl.ds(pl.multiple_of(me * width + h * DH, DH), DH)
                    rcv[half_of(piece, half), cols] = rows_of(n, half, h)

        for slot in range(2):
            send_q(slot).wait_recv()
            send_p(slot).wait_recv()

        @pl.loop(0, per)
        def _(piece):
            for slot in range(2):
                send_l(slot, piece).wait_recv()
                src = lax.rem(me + groups - 1 - 2 * slot, groups)
                cols = pl.ds(pl.multiple_of(src * width, DH), DH)
                for half in range(2):
                    at = half_of(piece, half)
                    value = dot(q_in[slot, at, :], p_in[slot], ((1,), (0,)))
                    rcv[at, cols] = (l_in[slot, at, :].astype(F32) + value).astype(BF16)

        load_gain.wait()

        @pl.loop(0, pieces)
        def _(i):
            piece, half = i // 2, lax.rem(i, 2)
            for d, skip in ((1, 1), (3, 1), (2, 0)):
                exchange(d, piece, half, skip, True).wait_recv()

            @pl.loop(0, HALF // 32)
            def _(j):
                at = pl.ds(pl.multiple_of(i * HALF + j * 32, 32), 32)
                wide = rcv[at, :].astype(F32)
                mean = jnp.mean(wide * wide, axis=-1, keepdims=True)
                out[at, :] = (wide * lax.rsqrt(mean + 1e-06) * gain[...]).astype(BF16)

        @pl.loop(0, pieces)
        def _(i):
            for d, skip in ((1, 1), (3, 1), (2, 0)):
                exchange(d, i // 2, lax.rem(i, 2), skip, False).wait_send()

        for slot in range(2):
            send_q(slot).wait_send()
            send_p(slot).wait_send()
            for piece in range(per):
                send_l(slot, piece).wait_send()

        all_of(0).wait_send()
        all_of(1).wait_send()

    return kernel


def solution(mesh):
    seqs, groups = mesh.shape["seq"], mesh.shape["head"]

    def shards(queries, keys, values, norm_gain):
        rows, width = queries.shape
        blocks = rows // BLK
        own = rows // groups
        per = own // BLK
        full = width * groups
        part = width // seqs
        dma = pltpu.SemaphoreType.DMA
        return pl.pallas_call(
            make_kernel(seqs, groups, rows, width),
            out_shape=pltpu.VMEM((own, full), BF16),
            in_specs=[pl.BlockSpec(memory_space=pl.ANY)] * 4,
            out_specs=pl.BlockSpec(memory_space=pltpu.VMEM),
            scratch_shapes=[
                pltpu.VMEM((rows, width), BF16),
                pltpu.VMEM((rows, width), BF16),
                pltpu.VMEM((rows, width), BF16),
                pltpu.VMEM((1, full), F32),
                pltpu.VMEM((blocks, width, DH), F32),
                pltpu.VMEM((width, DH), F32),
                pltpu.VMEM((seqs, part, DH), F32),
                pltpu.VMEM((seqs, part, DH), BF16),
                pltpu.VMEM((seqs, part, DH), BF16),
                pltpu.VMEM((rows, width), F32),
                pltpu.VMEM((rows, width), BF16),
                pltpu.VMEM((own, full), BF16),
                pltpu.VMEM((2, own, DH), BF16),
                pltpu.VMEM((2, own, DH), BF16),
                pltpu.VMEM((2, own, DH), BF16),
                pltpu.VMEM((2, own, DH), BF16),
                pltpu.VMEM((DH, DH), BF16),
                pltpu.VMEM((2, DH, DH), BF16),
                dma((3, blocks)),
                dma,
                dma((2,)),
                dma((2,)),
                dma((groups, own // HALF)),
                dma((groups, own // HALF)),
                dma((2, 2)),
                dma((2, 2, per)),
                dma((2, 2)),
            ],
            compiler_params=pltpu.CompilerParams(
                collective_id=0, has_side_effects=True, vmem_limit_bytes=48 << 20),
            name="attention_norm",
        )(queries, keys, values, norm_gain[None, :])

    return jax.shard_map(
        shards,
        mesh=mesh,
        in_specs=(P("seq", "head"), P("seq", "head"), P("seq", "head"), P()),
        out_specs=P(("seq", "head"), None),
        check_vma=False,
    )
```

time: 77.7 us -> 67.7 us (0.87)
  Pallas kernels: 72.7 us -> 64.8 us
  local copies, waits for them, and re-layouts: 4.79 us -> 2.71 us
    pallas_call x1, Pallas kernels: 72.7 us -> 64.8 us  [shards(): pl.pallas_call(make_kernel(seqs, groups, rows, width), out_shape=pltpu.VM...]
    unnamed x1 -> x3, local copies, waits for them, and re-layouts: 4.79 us -> 2.71 us
where the time goes in v2:
time: 67.7 us; the launch traced here: 67.6 us
  Pallas kernels  64.8 us (96%)
  local copies, waits for them, and re-layouts  2.71 us (4%)
    pallas_call x1, Pallas kernels, shards(): pl.pallas_call(make_kernel(seqs, groups, rows, width), out_shape=pltpu.VM...  64.8 us
    unnamed x3, local copies, waits for them, and re-layouts  2.71 us

profile of v2, /device:TPU:1, one launch (start us, length us, event | category | flops | bytes accessed | tf_op | source)
XLA Modules:
  0.0 67.6 jit_solution(2694543457210549334)
XLA Ops:
  0.0 0.0 copy-start
  0.0 0.7 %copy-done = f32[2048]{0:T(1024)S(1)} copy-done((f32[2048]{0:T(1024)S(1)}, f32[2048]{0:T(1024)}, u32[]{:S(2)}) %copy-start) | copy-done | bytes 8216
  0.7 64.8 %attention_norm.1 = bf16[1024,2048]{1,0:T(8,128)(2,1)S(1)} custom-call(bf16[4096,512]{1,0:T(8,128)(2,1)} %q_hbm.1, bf16[4096,512]{1,0:T(8,128)(2,1)} %k_hbm.1, bf16[4096,512]{1,0:T(8,128)(2,1)} %v_hbm.1, f32[1,2048]{1,0:T(1,128)S(1)} %bitcast.1), custom_call_target="tpu_custom_call" | custom-call | tf_op jit(solution)/shard_map/attention_norm/pallas_call | solution.py:320
  65.5 2.0 %copy.6 = bf16[1024,2048]{1,0:T(8,128)(2,1)} copy(bf16[1024,2048]{1,0:T(8,128)(2,1)S(1)} %attention_norm.1) | data formatting | bytes 8388608
Async XLA Ops:
  0.0 0.7 %copy-start = (f32[2048]{0:T(1024)S(1)}, f32[2048]{0:T(1024)}, u32[]{:S(2)}) copy-start(f32[2048]{0:T(1024)} %param.7) | copy-start | bytes 24580

commit v3 on v2

--- a/solution.py
+++ b/solution.py
@@ -8,6 +8,7 @@
 DH = 128
 BLK = 512
 HALF = BLK // 2
+PIECE = 128
 MESH = pl.DeviceIdType.MESH
 F32 = jnp.float32
 BF16 = jnp.bfloat16
@@ -38,13 +39,14 @@
     own = rows // groups
     part = (heads * DH) // seqs
     per = own // BLK
-    pieces = own // HALF
+    pieces = own // PIECE
+    cuts = HALF // PIECE
     side, steps = offsets(seqs)
     later = tuple(range(1, heads))
     every = tuple(range(heads))
 
     def kernel(q_hbm, k_hbm, v_hbm, g_hbm, out, q, k, v, gain, st, tot, got, pre, before, acc, att, rcv,
-               q_out, q_in, l_out, l_in, p_out, p_in,
+               q_in, l_out, l_in, p_out, p_in,
                in_sem, gain_sem, scan_send, scan_recv, send_sem, recv_sem, q_sems, l_sems, p_sems):
         me = lax.axis_index("head")
         my = lax.axis_index("seq")
@@ -62,24 +64,43 @@
         for n in range(blocks):
             load(0, n).start()
             load(1, n).start()
-        for n in range(blocks):
-            load(2, n).start()
         load_gain = pltpu.make_async_copy(g_hbm, gain, gain_sem)
         load_gain.start()
 
+        my_y, my_z, my_c = my // (2 * side), lax.rem(my // 2, side), lax.rem(my, 2)
+
+        def away(step):
+            y = lax.rem(my_y + step[0], side)
+            z = lax.rem(my_z + step[1], side)
+            return (y * side + z) * 2 + lax.rem(my_c + step[2], 2)
+
+        def first_block(d):
+            return lax.rem(me + d, groups) * per
+
         barrier = pltpu.get_barrier_semaphore()
-
-        @pl.loop(1, seqs)
-        def _(i):
-            pl.semaphore_signal(barrier, inc=1, device_id={"seq": lax.rem(my + i, seqs)}, device_id_type=MESH)
-
         for d in range(1, groups):
             pl.semaphore_signal(barrier, inc=1, device_id={"head": lax.rem(me + d, groups)}, device_id_type=MESH)
+        for step in steps:
+            pl.semaphore_signal(barrier, inc=1, device_id={"seq": away(step)}, device_id_type=MESH)
+
+        def ahead(src, dst, sems, slot, *which):
+            return pltpu.make_async_remote_copy(
+                src_ref=src, dst_ref=dst, send_sem=sems.at[(0, slot) + which], recv_sem=sems.at[(1, slot) + which],
+                device_id={"head": lax.rem(me + 1 + 2 * slot, groups)}, device_id_type=MESH)
+
+        def send_q(slot):
+            at = pl.ds(pl.multiple_of(first_block(1 + 2 * slot) * BLK, BLK), own)
+            return ahead(q_hbm.at[at, pl.ds(0, DH)], q_in.at[slot], q_sems, slot)
+
+        def send_l(slot, piece):
+            return ahead(l_out.at[slot, block(piece)], l_in.at[slot, block(piece)], l_sems, slot, piece)
+
+        def send_p(slot):
+            return ahead(p_out, p_in.at[slot], p_sems, slot)
 
         tot[...] = jnp.zeros_like(tot)
 
-        @pl.loop(0, blocks)
-        def _(n):
+        def gather(n):
             load(0, n).wait()
             load(1, n).wait()
             for h in range(heads):
@@ -89,17 +110,14 @@
                 st[n, hs, :] = run
                 tot[hs, :] = run + state
 
-        for n in range(blocks):
-            load(2, n).wait()
-
-        def first_block(d):
-            return lax.rem(me + d, groups) * per
+        pl.loop(0, 7)(gather)
+
+        pl.semaphore_wait(barrier, seqs - 1 + groups - 1)
 
         for slot in range(2):
-            at = pl.ds(pl.multiple_of(first_block(1 + 2 * slot) * BLK, BLK), own)
-            q_out[slot] = q[at, :DH]
-
-        pl.semaphore_wait(barrier, seqs - 1 + groups - 1)
+            send_q(slot).start()
+
+        pl.loop(7, blocks)(gather)
 
         def mine(i):
             return pl.ds(pl.multiple_of(i * part, part), part)
@@ -120,32 +138,11 @@
                 src_ref=ref, dst_ref=ref, send_sem=scan_send.at[stage], recv_sem=scan_recv.at[stage],
                 device_id={"seq": lax.rem(my + 1, seqs)}, device_id_type=MESH)
 
-        my_y, my_z, my_c = my // (2 * side), lax.rem(my // 2, side), lax.rem(my, 2)
-
-        def away(step):
-            y = lax.rem(my_y + step[0], side)
-            z = lax.rem(my_z + step[1], side)
-            return (y * side + z) * 2 + lax.rem(my_c + step[2], 2)
+        for n in range(blocks):
+            load(2, n).start()
 
         for step in steps:
             first(away(step)).start()
-
-        def ahead(src, dst, sems, slot, *which):
-            return pltpu.make_async_remote_copy(
-                src_ref=src, dst_ref=dst, send_sem=sems.at[(0, slot) + which], recv_sem=sems.at[(1, slot) + which],
-                device_id={"head": lax.rem(me + 1 + 2 * slot, groups)}, device_id_type=MESH)
-
-        def send_q(slot):
-            return ahead(q_out.at[slot], q_in.at[slot], q_sems, slot)
-
-        def send_l(slot, piece):
-            return ahead(l_out.at[slot, block(piece)], l_in.at[slot, block(piece)], l_sems, slot, piece)
-
-        def send_p(slot):
-            return ahead(p_out, p_in.at[slot], p_sems, slot)
-
-        for slot in range(2):
-            send_q(slot).start()
 
         got[my] = tot[mine(my), :]
 
@@ -164,6 +161,9 @@
             return (dot(s, v_lo, ((1,), (0,))),
                     dot(s_l, v_lo, ((1,), (0,))) + dot(s_h, v_hi, ((1,), (0,))))
 
+        for n in range(blocks):
+            load(2, n).wait()
+
         @pl.loop(0, 2 * per)
         def _(e):
             slot, piece = lax.rem(e, 2), e // 2
@@ -210,16 +210,15 @@
         for slot in range(2):
             send_p(slot).start()
 
-        def exchange(d, piece, half, skip, source):
+        def exchange(d, piece, skip, source):
             partner = lax.rem(me + (groups - d if source else d), groups)
             owner = partner if source else me
-            to = half_of(piece, half)
-            at = to if source else half_of(partner * per + piece, half)
+            to = pl.ds(pl.multiple_of(piece * PIECE, PIECE), PIECE)
+            at = to if source else pl.ds(pl.multiple_of(partner * own + piece * PIECE, PIECE), PIECE)
             cols = pl.ds(pl.multiple_of(owner * width + skip * DH, DH), width - skip * DH)
-            which = (d, piece * 2 + half)
             return pltpu.make_async_remote_copy(
                 src_ref=att.at[at, pl.ds(skip * DH, width - skip * DH)], dst_ref=rcv.at[to, cols],
-                send_sem=send_sem.at[which], recv_sem=recv_sem.at[which],
+                send_sem=send_sem.at[d, piece], recv_sem=recv_sem.at[d, piece],
                 device_id={"head": partner}, device_id_type=MESH)
 
         def rows_of(n, half, h):
@@ -233,7 +232,8 @@
             for half in range(2):
                 for h in which:
                     att[half_of(n, half), h * DH:(h + 1) * DH] = rows_of(n, half, h)
-                exchange(d, piece, half, which[0], False).start()
+                for cut in range(cuts):
+                    exchange(d, (piece * 2 + half) * cuts + cut, which[0], False).start()
 
         def finish_sides(piece):
             @pl.loop(0, 2)
@@ -278,13 +278,12 @@
 
         @pl.loop(0, pieces)
         def _(i):
-            piece, half = i // 2, lax.rem(i, 2)
             for d, skip in ((1, 1), (3, 1), (2, 0)):
-                exchange(d, piece, half, skip, True).wait_recv()
-
-            @pl.loop(0, HALF // 32)
+                exchange(d, i, skip, True).wait_recv()
+
+            @pl.loop(0, PIECE // 32)
             def _(j):
-                at = pl.ds(pl.multiple_of(i * HALF + j * 32, 32), 32)
+                at = pl.ds(pl.multiple_of(i * PIECE + j * 32, 32), 32)
                 wide = rcv[at, :].astype(F32)
                 mean = jnp.mean(wide * wide, axis=-1, keepdims=True)
                 out[at, :] = (wide * lax.rsqrt(mean + 1e-06) * gain[...]).astype(BF16)
@@ -292,7 +291,7 @@
         @pl.loop(0, pieces)
         def _(i):
             for d, skip in ((1, 1), (3, 1), (2, 0)):
-                exchange(d, i // 2, lax.rem(i, 2), skip, False).wait_send()
+                exchange(d, i, skip, False).wait_send()
 
         for slot in range(2):
             send_q(slot).wait_send()
@@ -320,7 +319,7 @@
         return pl.pallas_call(
             make_kernel(seqs, groups, rows, width),
             out_shape=pltpu.VMEM((own, full), BF16),
-            in_specs=[pl.BlockSpec(memory_space=pl.ANY)] * 4,
+            in_specs=[pl.BlockSpec(memory_space=pltpu.HBM)] * 4,
             out_specs=pl.BlockSpec(memory_space=pltpu.VMEM),
             scratch_shapes=[
                 pltpu.VMEM((rows, width), BF16),
@@ -338,21 +337,20 @@
                 pltpu.VMEM((2, own, DH), BF16),
                 pltpu.VMEM((2, own, DH), BF16),
                 pltpu.VMEM((2, own, DH), BF16),
-                pltpu.VMEM((2, own, DH), BF16),
                 pltpu.VMEM((DH, DH), BF16),
                 pltpu.VMEM((2, DH, DH), BF16),
                 dma((3, blocks)),
                 dma,
                 dma((2,)),
                 dma((2,)),
-                dma((groups, own // HALF)),
-                dma((groups, own // HALF)),
+                dma((groups, own // PIECE)),
+                dma((groups, own // PIECE)),
                 dma((2, 2)),
                 dma((2, 2, per)),
                 dma((2, 2)),
             ],
             compiler_params=pltpu.CompilerParams(
-                collective_id=0, has_side_effects=True, vmem_limit_bytes=48 << 20),
+                collective_id=0, has_side_effects=True, vmem_limit_bytes=58 << 20),
             name="attention_norm",
         )(queries, keys, values, norm_gain[None, :])
 

time: 67.7 us -> 66.7 us (0.985)
  local copies, waits for them, and re-layouts: 2.71 us -> 2.02 us
    unnamed x3 -> x1, local copies, waits for them, and re-layouts: 2.71 us -> 2.02 us
where the time goes in v3:
time: 66.7 us; the launch traced here: 66.6 us
  Pallas kernels  64.5 us (97%)
  local copies, waits for them, and re-layouts  2.02 us (3%)
    pallas_call x1, Pallas kernels, shards(): pl.pallas_call(make_kernel(seqs, groups, rows, width), out_shape=pltpu.VM...  64.5 us
    unnamed x1, local copies, waits for them, and re-layouts  2.02 us

profile of v3, /device:TPU:1, one launch (start us, length us, event | category | flops | bytes accessed | tf_op | source)
XLA Modules:
  0.0 66.6 jit_solution(8394872765859629727)
XLA Ops:
  0.0 64.5 %attention_norm.1 = bf16[1024,2048]{1,0:T(8,128)(2,1)S(1)} custom-call(bf16[4096,512]{1,0:T(8,128)(2,1)} %q_hbm.1, bf16[4096,512]{1,0:T(8,128)(2,1)} %k_hbm.1, bf16[4096,512]{1,0:T(8,128)(2,1)} %v_hbm.1, f32[1,2048]{1,0:T(1,128)} %bitcast.1), custom_call_target="tpu_custom_call" | custom-call | tf_op jit(solution)/shard_map/attention_norm/pallas_call | solution.py:319
  64.5 2.0 %copy.6 = bf16[1024,2048]{1,0:T(8,128)(2,1)} copy(bf16[1024,2048]{1,0:T(8,128)(2,1)S(1)} %attention_norm.1) | data formatting | bytes 8388608

commit v4 on v3

--- a/solution.py
+++ b/solution.py
@@ -52,7 +52,7 @@
         my = lax.axis_index("seq")
 
         def block(n):
-            return pl.ds(pl.multiple_of(n * BLK, BLK), BLK)
+            return pl.ds(n * BLK if isinstance(n, int) else pl.multiple_of(n * BLK, BLK), BLK)
 
         def half_of(n, half):
             return pl.ds(pl.multiple_of(n * BLK + half * HALF, HALF), HALF)
@@ -100,24 +100,25 @@
 
         tot[...] = jnp.zeros_like(tot)
 
-        def gather(n):
-            load(0, n).wait()
-            load(1, n).wait()
+        def gather(start, count):
+            for n in range(start, start + count):
+                load(0, n).wait()
+                load(1, n).wait()
+                load(2, n).start()
             for h in range(heads):
                 hs = slice(h * DH, (h + 1) * DH)
-                state = dot(k[block(n), hs], v[block(n), hs], ((0,), (0,)))
                 run = tot[hs, :]
-                st[n, hs, :] = run
-                tot[hs, :] = run + state
-
-        pl.loop(0, 7)(gather)
-
+                for n in range(start, start + count):
+                    st[n, hs, :] = run
+                    run = run + dot(k[block(n), hs], v[block(n), hs], ((0,), (0,)))
+                tot[hs, :] = run
+
+        gather(0, 4)
+        gather(4, 2)
         pl.semaphore_wait(barrier, seqs - 1 + groups - 1)
-
         for slot in range(2):
             send_q(slot).start()
-
-        pl.loop(7, blocks)(gather)
+        gather(6, 2)
 
         def mine(i):
             return pl.ds(pl.multiple_of(i * part, part), part)
@@ -137,9 +138,6 @@
             return pltpu.make_async_remote_copy(
                 src_ref=ref, dst_ref=ref, send_sem=scan_send.at[stage], recv_sem=scan_recv.at[stage],
                 device_id={"seq": lax.rem(my + 1, seqs)}, device_id_type=MESH)
-
-        for n in range(blocks):
-            load(2, n).start()
 
         for step in steps:
             first(away(step)).start()
@@ -164,15 +162,15 @@
         for n in range(blocks):
             load(2, n).wait()
 
-        @pl.loop(0, 2 * per)
-        def _(e):
-            slot, piece = lax.rem(e, 2), e // 2
-            n = first_block(1 + 2 * slot) + piece
-            low = st[n, :DH, :].astype(BF16)
-            for half, value in enumerate(local(n, 0)):
-                value = value + dot(q[half_of(n, half), :DH], low, ((1,), (0,)))
-                l_out[slot, half_of(piece, half), :] = value.astype(BF16)
-            send_l(slot, piece).start()
+        @pl.loop(0, per)
+        def _(piece):
+            for slot in range(2):
+                n = first_block(1 + 2 * slot) + piece
+                low = st[n, :DH, :].astype(BF16)
+                for half, value in enumerate(local(n, 0)):
+                    value = value + dot(q[half_of(n, half), :DH], low, ((1,), (0,)))
+                    l_out[slot, half_of(piece, half), :] = value.astype(BF16)
+                send_l(slot, piece).start()
 
         def keep(n, which):
             for h in which:
@@ -183,8 +181,6 @@
             @pl.loop(0, 2)
             def _(slot):
                 keep(first_block(1 + 2 * slot) + piece, later)
-
-        keep_sides(0)
 
         all_of(0).wait_recv()
         run = jnp.zeros((part, DH), F32)
@@ -197,6 +193,7 @@
 
         before[my] = pre[my]
 
+        keep_sides(0)
         keep(first_block(2), every)
 
         all_of(1).wait_recv()
@@ -240,15 +237,15 @@
             def _(slot):
                 finish(1 + 2 * slot, piece, later)
 
+        finish(2, 0, every)
         finish_sides(0)
-        finish(2, 0, every)
 
         @pl.loop(1, per)
         def _(piece):
+            keep(first_block(2) + piece, every)
+            finish(2, piece, every)
             keep_sides(piece)
             finish_sides(piece)
-            keep(first_block(2) + piece, every)
-            finish(2, piece, every)
 
         @pl.loop(0, per)
         def _(piece):

time: 66.7 us -> 66.6 us (level)
  no operation moved by 1% of the time
where the time goes in v4:
time: 66.6 us; the launch traced here: 66.5 us
  Pallas kernels  64.5 us (97%)
  local copies, waits for them, and re-layouts  2.02 us (3%)
    pallas_call x1, Pallas kernels, shards(): pl.pallas_call(make_kernel(seqs, groups, rows, width), out_shape=pltpu.VM...  64.5 us
    unnamed x1, local copies, waits for them, and re-layouts  2.02 us

profile of v4, /device:TPU:1, one launch (start us, length us, event | category | flops | bytes accessed | tf_op | source)
XLA Modules:
  0.0 66.5 jit_solution(484938992423474059)
XLA Ops:
  0.0 64.5 %attention_norm.1 = bf16[1024,2048]{1,0:T(8,128)(2,1)S(1)} custom-call(bf16[4096,512]{1,0:T(8,128)(2,1)} %q_hbm.1, bf16[4096,512]{1,0:T(8,128)(2,1)} %k_hbm.1, bf16[4096,512]{1,0:T(8,128)(2,1)} %v_hbm.1, f32[1,2048]{1,0:T(1,128)} %bitcast.1), custom_call_target="tpu_custom_call" | custom-call | tf_op jit(solution)/shard_map/attention_norm/pallas_call | solution.py:316
  64.5 2.0 %copy.6 = bf16[1024,2048]{1,0:T(8,128)(2,1)} copy(bf16[1024,2048]{1,0:T(8,128)(2,1)S(1)} %attention_norm.1) | data formatting | bytes 8388608

commit v5 on v4

--- a/solution.py
+++ b/solution.py
@@ -271,33 +271,36 @@
                     value = dot(q_in[slot, at, :], p_in[slot], ((1,), (0,)))
                     rcv[at, cols] = (l_in[slot, at, :].astype(F32) + value).astype(BF16)
 
+        for slot in range(2):
+            send_q(slot).wait_send()
+            send_p(slot).wait_send()
+            for piece in range(per):
+                send_l(slot, piece).wait_send()
+
+        all_of(0).wait_send()
+        all_of(1).wait_send()
+
         load_gain.wait()
 
         @pl.loop(0, pieces)
         def _(i):
+            @pl.when(i > 0)
+            def _():
+                for d, skip in ((1, 1), (3, 1), (2, 0)):
+                    exchange(d, i - 1, skip, False).wait_send()
+
             for d, skip in ((1, 1), (3, 1), (2, 0)):
                 exchange(d, i, skip, True).wait_recv()
 
-            @pl.loop(0, PIECE // 32)
+            @pl.loop(0, PIECE // 32, unroll=PIECE // 32)
             def _(j):
                 at = pl.ds(pl.multiple_of(i * PIECE + j * 32, 32), 32)
                 wide = rcv[at, :].astype(F32)
                 mean = jnp.mean(wide * wide, axis=-1, keepdims=True)
                 out[at, :] = (wide * lax.rsqrt(mean + 1e-06) * gain[...]).astype(BF16)
 
-        @pl.loop(0, pieces)
-        def _(i):
-            for d, skip in ((1, 1), (3, 1), (2, 0)):
-                exchange(d, i, skip, False).wait_send()
-
-        for slot in range(2):
-            send_q(slot).wait_send()
-            send_p(slot).wait_send()
-            for piece in range(per):
-                send_l(slot, piece).wait_send()
-
-        all_of(0).wait_send()
-        all_of(1).wait_send()
+        for d, skip in ((1, 1), (3, 1), (2, 0)):
+            exchange(d, pieces - 1, skip, False).wait_send()
 
     return kernel
 

time: 66.6 us -> 66.2 us (level)
  no operation moved by 1% of the time
where the time goes in v5:
time: 66.2 us; the launch traced here: 66.1 us
  Pallas kernels  64.1 us (97%)
  local copies, waits for them, and re-layouts  2.02 us (3%)
    pallas_call x1, Pallas kernels, shards(): pl.pallas_call(make_kernel(seqs, groups, rows, width), out_shape=pltpu.VM...  64.1 us
    unnamed x1, local copies, waits for them, and re-layouts  2.02 us

profile of v5, /device:TPU:1, one launch (start us, length us, event | category | flops | bytes accessed | tf_op | source)
XLA Modules:
  0.0 66.1 jit_solution(5509920885023166395)
XLA Ops:
  0.0 64.1 %attention_norm.1 = bf16[1024,2048]{1,0:T(8,128)(2,1)S(1)} custom-call(bf16[4096,512]{1,0:T(8,128)(2,1)} %q_hbm.1, bf16[4096,512]{1,0:T(8,128)(2,1)} %k_hbm.1, bf16[4096,512]{1,0:T(8,128)(2,1)} %v_hbm.1, f32[1,2048]{1,0:T(1,128)} %bitcast.1), custom_call_target="tpu_custom_call" | custom-call | tf_op jit(solution)/shard_map/attention_norm/pallas_call | solution.py:319
  64.1 2.0 %copy.6 = bf16[1024,2048]{1,0:T(8,128)(2,1)} copy(bf16[1024,2048]{1,0:T(8,128)(2,1)S(1)} %attention_norm.1) | data formatting | bytes 8388608

commit v6 on v5

--- a/solution.py
+++ b/solution.py
@@ -113,7 +113,8 @@
                     run = run + dot(k[block(n), hs], v[block(n), hs], ((0,), (0,)))
                 tot[hs, :] = run
 
-        gather(0, 4)
+        gather(0, 2)
+        gather(2, 2)
         gather(4, 2)
         pl.semaphore_wait(barrier, seqs - 1 + groups - 1)
         for slot in range(2):

time: 66.2 us -> 66.2 us (level)
  no operation moved by 1% of the time
where the time goes in v6:
time: 66.2 us; the launch traced here: 66.1 us
  Pallas kernels  64.1 us (97%)
  local copies, waits for them, and re-layouts  2.02 us (3%)
    pallas_call x1, Pallas kernels, shards(): pl.pallas_call(make_kernel(seqs, groups, rows, width), out_shape=pltpu.VM...  64.1 us
    unnamed x1, local copies, waits for them, and re-layouts  2.02 us

profile of v6, /device:TPU:1, one launch (start us, length us, event | category | flops | bytes accessed | tf_op | source)
XLA Modules:
  0.0 66.1 jit_solution(13040856253094172549)
XLA Ops:
  0.0 64.1 %attention_norm.1 = bf16[1024,2048]{1,0:T(8,128)(2,1)S(1)} custom-call(bf16[4096,512]{1,0:T(8,128)(2,1)} %q_hbm.1, bf16[4096,512]{1,0:T(8,128)(2,1)} %k_hbm.1, bf16[4096,512]{1,0:T(8,128)(2,1)} %v_hbm.1, f32[1,2048]{1,0:T(1,128)} %bitcast.1), custom_call_target="tpu_custom_call" | custom-call | tf_op jit(solution)/shard_map/attention_norm/pallas_call | solution.py:320
  64.1 2.0 %copy.6 = bf16[1024,2048]{1,0:T(8,128)(2,1)} copy(bf16[1024,2048]{1,0:T(8,128)(2,1)S(1)} %attention_norm.1) | data formatting | bytes 8388608
